TPU v7x, 256 devices: a whole 4x4x8 slice. The times are simulated.
256 devices in a mesh: row: 16 (over y, x), col: 16 (over z, core).
Axes of the slice: x: 4, y: 4, z: 8, core: 2. Of those that a mesh axis runs over, the one named last changes fastest.
Arguments:
- g0_values: bfloat16 [8192, 8192], P('row', 'col'), may hold values from -6 to 6
- g0_pattern: int32 [64, 64], P('row', 'col'), may hold values 0 or 1
- sigma_values: bfloat16 [16, 96, 128, 128], P('row', 'col'), may hold values from -0.0014648438 to 0.0014648438
- sigma_pairs: int32 [16, 96, 2], P('row', 'col'), may hold values from 0 to 63, as said below
- sigma_count: int32 [16, 16], P('row', 'col'), may hold values from 1 to 6, as said below
Outputs:
- g_full: bfloat16 [8192, 8192], P('row', 'col')
Inputs may be any that keep to these rules, and one draw needn't show every extreme that they name: `sigma_pairs`: slot pairs of the device at position (g, o) name blocks with block row in g * 4 to g * 4 + 3 and block column in o * 4 to o * 4 + 3; the pairs of one device are distinct. `sigma_count`: count of live slots, which are the first ones of a device.
All inputs are finite; a program needn't handle non-finite values. No bound on the sum of `g0_pattern` on one device may be relied on, other than what follows from the above.
Results may differ from a plain program's by a relative error of at most 0.0037.
Values may be sent and summed in bfloat16 or wider, within the bound.
A program may use at most 128 MiB of HBM per device.

v0:
```python
import jax
import jax.numpy as jnp
from jax import lax
from jax.sharding import PartitionSpec as P


def per_device(g0_values, g0_pattern, sigma_values, sigma_pairs, sigma_count):
    block_rows = g0_pattern.shape[0]
    block_cols = g0_pattern.shape[1]
    width = sigma_values.shape[-1]
    slot_total = sigma_values.shape[1]
    mask = jnp.repeat(jnp.repeat(g0_pattern, width, axis=0), width, axis=1)
    g0_tile = g0_values * mask.astype(jnp.bfloat16)
    panel = lax.all_gather(g0_tile, "col", axis=1, tiled=True)
    live = jnp.arange(slot_total, dtype=jnp.int32) < sigma_count[0, 0]
    local_k = jnp.where(live, sigma_pairs[0, :, 0] % block_rows, block_rows)
    local_j = sigma_pairs[0, :, 1] % block_cols
    dense = jnp.zeros((block_rows, width, block_cols, width), jnp.bfloat16)
    dense = dense.at[local_k, :, local_j, :].add(sigma_values[0], mode="drop")
    sigma_tile = dense.reshape(block_rows * width, block_cols * width)
    columns = panel
    left_sum = jnp.dot(
        columns,
        lax.all_gather(sigma_tile, "row", axis=0, tiled=True),
        preferred_element_type=jnp.float32,
    )
    left_tile = left_sum.astype(jnp.bfloat16)
    start_value = g0_tile.astype(jnp.float32)
    left_panel = lax.all_gather(left_tile, "col", axis=1, tiled=True)
    columns = left_panel
    result = start_value + jnp.dot(
        columns,
        lax.all_gather(g0_tile, "row", axis=0, tiled=True),
        preferred_element_type=jnp.float32,
    )
    return result.astype(jnp.bfloat16)


def solution(mesh):
    placed = (
        P("row", "col"),
        P("row", "col"),
        P("row", "col", None, None),
        P("row", "col", None),
        P("row", "col"),
    )
    return jax.shard_map(
        per_device, mesh=mesh, in_specs=placed, out_specs=P("row", "col"), check_vma=False
    )
```

profile of v0, /device:TPU:1, one launch (start us, length us, event | category | flops | bytes accessed | tf_op | source)
XLA Modules:
  0.0 299.8 jit_solution(1443495275628197058)
XLA Ops:
  6.5 0.0 all-gather.5.cloned.1.call-start
  6.5 0.7 convert_element_type.20
  7.2 0.6 broadcast_in_dim.14
  7.9 1.9 bitcast_multiply_fusion
  9.8 0.0 all-gather.5.cloned.1.call-update
  9.8 0.0 all-gather.7.cloned.1.call-start
  10.5 0.8 fusion.4
  11.3 0.1 broadcast_in_dim.15
  11.4 2.0 scatter_fusion
  13.4 0.4 copy.6
  13.8 0.9 copy.11
  14.7 0.0 all-gather.7.cloned.1.call-update
  14.7 0.0 all-gather.11.cloned.1.call-start
  14.8 0.7 all-gather.11.cloned.1.call-update
  15.5 0.0 copy-start
  15.5 0.0 all-gather.9.cloned.1.call-start
  15.5 54.6 %all-gather.5.cloned.1.call-done = bf16[512,8192]{1,0:T(8,128)(2,1)} async-done(((bf16[512,512]{1,0:T(8,128)(2,1)}), bf16[512,8192]{1,0:T(8,128)(2,1)}) %all-gather.5.cloned.1.call-update) | async-done | bytes 8388624 | tf_op jit(solution)/shard_map/all_gather | solution.py:14
  70.1 76.4 %all-gather.7.cloned.1.call-done = bf16[8192,512]{1,0:T(8,128)(2,1)} async-done(((bf16[512,512]{1,0:T(8,128)(2,1)}), bf16[8192,512]{1,0:T(8,128)(2,1)}) %all-gather.7.cloned.1.call-update) | async-done | bytes 8388624 | tf_op jit(solution)/shard_map/all_gather | solution.py:24
  146.4 11.1 %convolution_convert_fusion = bf16[512,512]{1,0:T(8,128)(2,1)} fusion(bf16[512,8192]{1,0:T(8,128)(2,1)} %all-gather.5.cloned.1.call-done, bf16[8192,512]{1,0:T(8,128)(2,1)} %all-gather.7.cloned.1.call-done), kind=kOutput, calls=%fused_computation.3 | convolution fusion | flops 4295229440 | bytes 17301504 | tf_op jit(solution)/shard_map/dot_general | solution.py:22
  157.5 0.0 all-gather.9.cloned.1.call-update
  157.5 66.9 %all-gather.11.cloned.1.call-done = bf16[8192,512]{1,0:T(8,128)(2,1)} async-done(((bf16[512,512]{1,0:T(8,128)(2,1)}), bf16[8192,512]{1,0:T(8,128)(2,1)}) %all-gather.11.cloned.1.call-update) | async-done | bytes 8388624 | tf_op jit(solution)/shard_map/all_gather | solution.py:33
  224.4 57.8 %all-gather.9.cloned.1.call-done = bf16[512,8192]{1,0:T(8,128)(2,1)} async-done(((bf16[512,512]{1,0:T(8,128)(2,1)}), bf16[512,8192]{1,0:T(8,128)(2,1)}) %all-gather.9.cloned.1.call-update) | async-done | bytes 8388624 | tf_op jit(solution)/shard_map/all_gather | solution.py:29
  282.2 0.0 copy-done
  282.2 11.0 %fusion = bf16[512,512]{1,0:T(8,128)(2,1)} fusion(bf16[512,8192]{1,0:T(8,128)(2,1)} %all-gather.9.cloned.1.call-done, bf16[8192,512]{1,0:T(8,128)(2,1)} %all-gather.11.cloned.1.call-done, bf16[512,512]{1,0:T(8,128)(2,1)S(1)} %copy-done), kind=kOutput, calls=%fused_computation.2 | convolution fusion | flops 4295753728 | bytes 17825792 | tf_op jit(solution)/shard_map/dot_general | solution.py:31
  (1 shorter events, 0.0 us)
Async XLA Ops:
  6.5 63.5 %all-gather.5.cloned.1.call-start = ((), (), s32[]{:S(2)}) async-start(), calls=%async_computation | async-start | bytes 8912896 | tf_op jit(solution)/shard_map/all_gather | solution.py:14
  9.8 136.7 %all-gather.7.cloned.1.call-start = ((), (), s32[]{:S(2)}) async-start(), calls=%async_computation.1 | async-start | bytes 8912896 | tf_op jit(solution)/shard_map/all_gather | solution.py:24
  14.7 209.7 %all-gather.11.cloned.1.call-start = ((), (), s32[]{:S(2)}) async-start(), calls=%async_computation.3 | async-start | bytes 8912896 | tf_op jit(solution)/shard_map/all_gather | solution.py:33
  15.5 266.8 %copy-start = (bf16[512,512]{1,0:T(8,128)(2,1)S(1)}, bf16[512,512]{1,0:T(8,128)(2,1)}, u32[]{:S(2)}) copy-start(bf16[512,512]{1,0:T(8,128)(2,1)} %bitcast_multiply_fusion) | copy-start | bytes 1572868
  15.5 266.7 %all-gather.9.cloned.1.call-start = ((), (), s32[]{:S(2)}) async-start(), calls=%async_computation.2 | async-start | bytes 8912896 | tf_op jit(solution)/shard_map/all_gather | solution.py:29
Sparse Core Ops, SparseCore 0:
  9.9 60.1 all-gather.4
  72.5 73.8 all-gather.6
  148.9 75.4 all-gather.10
  226.1 56.0 all-gather.8
where the time goes:
time: 300 us
  waiting for transfers between devices  256 us (85%)
  matrix products  22.1 us (7%)
  between operations  13.8 us (5%)
  other arithmetic  5.36 us (2%)
    all_gather x1, waiting for transfers between devices, per_device(): lax.all_gather(sigma_tile, 'row', axis=0, tiled=True)  76.4 us
    all_gather x1, waiting for transfers between devices, per_device(): lax.all_gather(g0_tile, 'row', axis=0, tiled=True)  66.9 us
    all_gather x1, waiting for transfers between devices, per_device(): left_panel = lax.all_gather(left_tile, 'col', axis=1, tiled=True)  57.8 us
    all_gather x1, waiting for transfers between devices, per_device(): panel = lax.all_gather(g0_tile, 'col', axis=1, tiled=True)  54.6 us
    dot_general x1, matrix products, per_device(): jnp.dot(columns, lax.all_gather(sigma_tile, 'row', axis=0, tiled=True), p...  11.1 us
    dot_general x1, matrix products, per_device(): jnp.dot(columns, lax.all_gather(g0_tile, 'row', axis=0, tiled=True), pref...  11 us
  transfers between devices with their start and end apart: 4, of which 4 were waited for; matrix products, arithmetic and copies ran while one was open for 5% of the time, Pallas kernels for 0%

commit v1 on v0

v1 whole, which is shorter than its diff:
```python
import functools
import heapq

import jax
import jax.numpy as jnp
from jax import lax
from jax.experimental import pallas as pl
from jax.experimental.pallas import tpu as pltpu
from jax.sharding import PartitionSpec as P

MESH = pl.DeviceIdType.MESH
NX, NY, NZ = 4, 4, 8
ROWS = NX * NY
COLS = NZ * 2
CH = 2
SLOT_ROWS = 832

LINK = 47.0e3
CORE = 400.0e3
HOP = 1.5


def kernel(
    g0_ref, sig_ref, pat_ref, pairs_ref, count_ref, out_ref,
    gr, gc, lr, sc, sd, lacc, cacc, send_sems, recv_sems,
):
    tile = g0_ref.shape[0]
    width = sig_ref.shape[1]
    nblk = tile // width
    slots = sig_ref.shape[0] // width
    ch_rows = tile // CH
    row = lax.axis_index("row")
    col = lax.axis_index("col")
    x, y = lax.rem(row, NX), row // NX
    z, c = col // 2, lax.rem(col, 2)

    def wrap(v, n):
        return lax.rem(v + n, n)

    def device(dx=0, dy=0, dz=0, dc=0):
        xx, yy, zz = wrap(x + dx, NX), wrap(y + dy, NY), wrap(z + dz, NZ)
        cc = 1 - c if dc else c
        return (yy * NX + xx, zz * 2 + cc)

    barrier = pltpu.get_barrier_semaphore()
    near = [device(dx=1), device(dx=-1), device(dy=1), device(dy=-1), device(dz=1), device(dz=-1), device(dc=1)]
    for d in near:
        pl.semaphore_signal(barrier, inc=1, device_id=d, device_id_type=MESH)

    for a in range(nblk):
        for b in range(nblk):
            ra, rb = pl.ds(a * width, width), pl.ds(b * width, width)
            block = g0_ref[ra, rb]
            block = jnp.where(pat_ref[a, b] != 0, block, jnp.zeros_like(block))
            gc[row, ra, rb] = block
            h, off = divmod(a * width, ch_rows)
            gr[h, col, pl.ds(off, width), rb] = block
            cacc[h, pl.ds(off, width), rb] = block.astype(jnp.float32)

    sc[row, pl.ds(0, slots * width), :] = sig_ref[...]
    place = lax.broadcasted_iota(jnp.int32, (nblk * nblk, width), 0)
    table = jnp.full((nblk * nblk, width), -1.0, jnp.float32)
    for s in range(slots):
        at = lax.rem(pairs_ref[s, 0], nblk) * nblk + lax.rem(pairs_ref[s, 1], nblk)
        at = jnp.where(s < count_ref[0, 0], at, -1)
        table = jnp.where(place == at, float(s), table)
    sc[row, pl.ds(slots * width, nblk * nblk), :] = table.astype(jnp.bfloat16)
    tail = slots * width + nblk * nblk
    sc[row, pl.ds(tail, SLOT_ROWS - tail), :] = jnp.zeros((SLOT_ROWS - tail, width), jnp.bfloat16)

    pl.semaphore_wait(barrier, len(near))

    waits = {}
    sends = []
    state = {"now": 0.0, "seq": 0, "done": set()}
    link_free = {}
    heap = []
    actions = {}
    pending = []
    ids = {}

    def push(time, kind, name):
        state["seq"] += 1
        heapq.heappush(heap, (time, kind, state["seq"], name))

    def send(name, src, dst, link, dev, nbytes, landed, after):
        i = ids.setdefault(name, len(ids))
        copy = pltpu.make_async_remote_copy(
            src_ref=src, dst_ref=dst, send_sem=send_sems.at[i], recv_sem=recv_sems.at[i],
            device_id=dev, device_id_type=MESH,
        )
        copy.start()
        sends.append(copy)
        rate = CORE if link == "c" else LINK
        t = max(state["now"], link_free.get(link, 0.0)) + nbytes / rate
        link_free[link] = t

        def act():
            pltpu.make_async_remote_copy(
                src_ref=landed, dst_ref=landed, send_sem=send_sems.at[i], recv_sem=recv_sems.at[i],
                device_id=dev, device_id_type=MESH,
            ).wait_recv()
            if after is not None:
                after()

        actions[name] = (act, 0.05)
        push(t + HOP, 0, name)

    def step(name, needs, fn, cost):
        actions[name] = (fn, cost)
        pending.append((set(needs), name))

    def settle():
        for item in list(pending):
            if item[0] <= state["done"]:
                pending.remove(item)
                push(state["now"], 1, item[1])

    def run():
        settle()
        while heap:
            ready = [e for e in heap if e[0] <= state["now"]]
            e = min(ready, key=lambda e: (e[1], e[0], e[2])) if ready else heap[0]
            heap.remove(e)
            heapq.heapify(heap)
            fn, cost = actions[e[3]]
            state["now"] = max(state["now"], e[0]) + cost
            fn()
            state["done"].add(e[3])
            settle()
        assert not pending, pending

    def z_stream(tag, buf, h):
        half = ch_rows // 2
        nbytes = ch_rows * tile * 2

        def piece(zz, cc, part):
            r = buf.at[h, wrap(zz, NZ) * 2 + cc]
            return r if part is None else r.at[pl.ds(part * half, half), :]

        def to_core(name, zz, part):
            src = piece(zz, c, part)
            n = nbytes if part is None else nbytes // 2
            send(name, src, src, "c", device(dc=1), n, piece(zz, 1 - c, part), None)

        def hop(direction, k):
            part = None if k < NZ // 2 else (0 if direction > 0 else 1)
            src = piece(z - direction * (k - 1), c, part)
            n = nbytes if part is None else nbytes // 2

            def after():
                if k < NZ // 2:
                    hop(direction, k + 1)
                to_core((tag, "c", h, direction, k), z - direction * k, part)

            send((tag, "z", h, direction, k), src, src, ("z", direction), device(dz=direction), n,
                 piece(z - direction * k, c, part), after)

        hop(1, 1)
        hop(-1, 1)
        to_core((tag, "c", h, 0, 0), z, None)

    def z_needs(tag, h, k):
        if k == 0:
            return [(tag, "c", h, 0, 0)]
        return [(tag, s, h, d, k) for s in ("z", "c") for d in (1, -1)]

    def xy_stream(tag, buf, rows, nbytes):
        q = rows // 4
        names = []

        def piece(dx, dy, half, part):
            r = buf.at[wrap(y + dy, NY) * NX + wrap(x + dx, NX)]
            if part is None:
                return r.at[pl.ds(half * 2 * q, 2 * q), :]
            return r.at[pl.ds((half * 2 + part) * q, q), :]

        def off(half, first, second):
            return (first, second) if half == 0 else (second, first)

        def second_phase(half, at):
            axis = "y" if half == 0 else "x"

            def hop(direction, k):
                part = None if k == 1 else (0 if direction > 0 else 1)
                src = piece(*off(half, at, -direction * (k - 1)), half, part)
                land = piece(*off(half, at, -direction * k), half, part)
                n = nbytes // 2 if k == 1 else nbytes // 4
                name = (tag, half, 2, at, direction, k)
                names.append(name)
                send(name, src, src, (axis, direction), device(**{"d" + axis: direction}), n, land,
                     (lambda: hop(direction, 2)) if k == 1 else None)

            hop(1, 1)
            hop(-1, 1)

        def first_phase(half):
            axis = "x" if half == 0 else "y"
            far = []

            def hop(direction, k):
                part = None if k == 1 else (0 if direction > 0 else 1)
                src = piece(*off(half, -direction * (k - 1), 0), half, part)
                land = piece(*off(half, -direction * k, 0), half, part)
                n = nbytes // 2 if k == 1 else nbytes // 4
                name = (tag, half, 1, direction, k)
                names.append(name)

                def after():
                    if k == 1:
                        hop(direction, 2)
                        second_phase(half, -direction)
                    else:
                        far.append(direction)
                        if len(far) == 2:
                            second_phase(half, 2)

                send(name, src, src, (axis, direction), device(**{"d" + axis: direction}), n, land, after)

            hop(1, 1)
            hop(-1, 1)

        for half in (0, 1):
            first_phase(half)
        for half in (0, 1):
            second_phase(half, 0)
        return 80 // 2

    def xy_all(tag):
        need = []
        for half in (0, 1):
            for d in (1, -1):
                for k in (1, 2):
                    need.append((tag, half, 1, d, k))
                    need.extend((tag, half, 2, at, d, k) for at in (0, 1, -1, 2))
        return need

    def expand(first, n):
        @pl.loop(first, first + n)
        def _(r):
            t = sc[r, pl.ds(slots * width, nblk * nblk), :].astype(jnp.float32)
            for b in range(nblk * nblk):
                line = t[b : b + 1, :]
                total = jnp.zeros((width, width), jnp.bfloat16)
                for s in range(slots):
                    on = jnp.where(line == float(s), 1.0, 0.0).astype(jnp.bfloat16)
                    total = total + sc[r, pl.ds(s * width, width), :] * on
                sd[r, pl.ds((b // nblk) * width, width), pl.ds((b % nblk) * width, width)] = total

    def dots(acc, left_buf, right_buf, h, k):
        far = NZ // 2
        n = 2 if k in (0, far) else 4

        @pl.loop(0, n)
        def _(i):
            cc = lax.rem(i, 2)
            sign = 1 - 2 * (i // 2)
            t = wrap(z + sign * k, NZ) * 2 + cc
            acc[h] += jnp.dot(left_buf[h, t], right_buf[t], preferred_element_type=jnp.float32)

    def finish_left(h):
        lr[h, col] = lacc[h].astype(jnp.bfloat16)
        z_stream("L", lr, h)

    def finish(h):
        out_ref[pl.ds(h * ch_rows, ch_rows), :] = cacc[h].astype(jnp.bfloat16)

    lacc[...] = jnp.zeros_like(lacc)
    xy_stream("S", sc, SLOT_ROWS, SLOT_ROWS * width * 2)
    for h in range(CH):
        z_stream("G", gr, h)
    xy_stream("C", gc, tile, tile * tile * 2)

    group = 4
    for i in range(ROWS // group):
        step(("expand", i), xy_all("S") + ([("expand", i - 1)] if i else []), functools.partial(expand, i * group, group), 1.0)
    last = ("expand", ROWS // group - 1)
    far = NZ // 2
    for h in range(CH):
        for k in range(far + 1):
            step(("left", h, k), z_needs("G", h, k) + [last], functools.partial(dots, lacc, gr, sd, h, k), 1.0)
            step(("prod", h, k), z_needs("L", h, k) + xy_all("C") + [("left done", h)],
                 functools.partial(dots, cacc, lr, gc, h, k), 1.0)
        step(("left done", h), [("left", h, k) for k in range(far + 1)], functools.partial(finish_left, h), 0.3)
        step(("done", h), [("prod", h, k) for k in range(far + 1)], functools.partial(finish, h), 0.3)
    run()
    for copy in sends:
        copy.wait_send()
    assert len(ids) == N_COPIES, len(ids)


N_COPIES = 2 * 40 + 2 * CH * (2 * (NZ // 2) * 2 + 1)


def per_device(g0_values, g0_pattern, sigma_values, sigma_pairs, sigma_count):
    tile = g0_values.shape[0]
    _, slots, width, _ = sigma_values.shape
    bf, f32 = jnp.bfloat16, jnp.float32
    vmem = pl.BlockSpec(memory_space=pltpu.VMEM)
    smem = pl.BlockSpec(memory_space=pltpu.SMEM)
    return pl.pallas_call(
        kernel,
        name="dyson",
        out_shape=jax.ShapeDtypeStruct((tile, tile), bf),
        in_specs=[vmem, vmem, smem, smem, smem],
        out_specs=vmem,
        scratch_shapes=[
            pltpu.VMEM((CH, COLS, tile // CH, tile), bf),
            pltpu.VMEM((ROWS, tile, tile), bf),
            pltpu.VMEM((CH, COLS, tile // CH, tile), bf),
            pltpu.VMEM((ROWS, SLOT_ROWS, width), bf),
            pltpu.VMEM((ROWS, tile, tile), bf),
            pltpu.VMEM((CH, tile // CH, tile), f32),
            pltpu.VMEM((CH, tile // CH, tile), f32),
            pltpu.SemaphoreType.DMA((N_COPIES,)),
            pltpu.SemaphoreType.DMA((N_COPIES,)),
        ],
        compiler_params=pltpu.CompilerParams(
            collective_id=0, has_side_effects=True, vmem_limit_bytes=58 << 20
        ),
    )(
        g0_values,
        sigma_values.reshape(slots * width, width),
        g0_pattern,
        sigma_pairs.reshape(slots, 2),
        sigma_count,
    )


def solution(mesh):
    placed = (
        P("row", "col"),
        P("row", "col"),
        P("row", "col", None, None),
        P("row", "col", None),
        P("row", "col"),
    )
    return jax.shard_map(
        per_device, mesh=mesh, in_specs=placed, out_specs=P("row", "col"), check_vma=False
    )
```

time: 300 us -> 137 us (0.46)
  waiting for transfers between devices: 256 us -> 0 us
  Pallas kernels: 0 us -> 133 us
  matrix products: 22.1 us -> 0 us
  between operations: 13.8 us -> 0.67 us
  other arithmetic: 5.36 us -> 0 us
    all_gather x4 -> x0, waiting for transfers between devices: 256 us -> none  [the longest x1 76.4 us: per_device(): lax.all_gather(sigma_tile, 'row', axis=0, tiled=True)]
    pallas_call x0 -> x1, Pallas kernels: none -> 133 us  [per_device(): pl.pallas_call(kernel, name='dyson', out_shape=jax.ShapeDtypeStruct((tile...]
    dot_general x2 -> x0, matrix products: 22.1 us -> none  [the longest x1 11.1 us: per_device(): jnp.dot(columns, lax.all_gather(sigma_tile, 'row', axis=0, tiled=True), p...]
  transfers between devices with their start and end apart: 4 -> 0, of which waited for: 4 -> 0; matrix products, arithmetic and copies ran while one was open for 5% -> 0% of each run, Pallas kernels for 0% -> 0%
where the time goes in v1:
time: 137 us
  Pallas kernels  133 us (97%)
  local copies, waits for them, and re-layouts  3.22 us (2%)
    pallas_call x1, Pallas kernels, per_device(): pl.pallas_call(kernel, name='dyson', out_shape=jax.ShapeDtypeStruct((tile...  133 us

profile of v1, /device:TPU:1, one launch (start us, length us, event | category | flops | bytes accessed | tf_op | source)
XLA Modules:
  0.0 136.7 jit_solution(11137294918717948203)
XLA Ops:
  0.7 0.0 copy-start
  0.7 0.7 copy-done
  1.3 0.7 copy.6.pairs_ref
  2.0 132.8 %dyson.1 = bf16[512,512]{1,0:T(8,128)(2,1)} custom-call(bf16[512,512]{1,0:T(8,128)(2,1)} %g0_ref.1, bf16[768,128]{1,0:T(8,128)(2,1)} %bitcast.2, s32[4,4]{1,0:T(4,128)} %pat_ref.1, s32[6,2]{1,0:T(8,128)} %copy.6.pairs_ref, s32[1,1]{1,0:T(1,128)S(6)} %copy.8.count_ref), custom_call_target="tpu_custom_call" | custom-call | tf_op jit(solution)/shard_map/dyson/pallas_call | solution.py:301
  134.8 1.9 %copy.9 = bf16[512,512]{1,0:T(8,128)(2,1)} copy(bf16[512,512]{1,0:T(8,128)(2,1)} %dyson.1) | data formatting | bytes 1048576
Async XLA Ops:
  0.7 0.7 copy-start

commit v2 on v1

--- a/solution.py
+++ b/solution.py
@@ -15,9 +15,9 @@
 CH = 2
 SLOT_ROWS = 832
 
-LINK = 47.0e3
-CORE = 400.0e3
+RATE = {"x": 40.0e3, "y": 40.0e3, "z": 46.0e3, "c": 250.0e3}
 HOP = 1.5
+WINDOW = {"x": 2, "y": 2, "z": 99, "c": 99}
 
 
 def kernel(
@@ -53,15 +53,14 @@
             block = g0_ref[ra, rb]
             block = jnp.where(pat_ref[a, b] != 0, block, jnp.zeros_like(block))
             gc[row, ra, rb] = block
-            h, off = divmod(a * width, ch_rows)
-            gr[h, col, pl.ds(off, width), rb] = block
-            cacc[h, pl.ds(off, width), rb] = block.astype(jnp.float32)
+            gr[col, ra, rb] = block
+            cacc[ra, rb] = block.astype(jnp.float32)
 
     sc[row, pl.ds(0, slots * width), :] = sig_ref[...]
     place = lax.broadcasted_iota(jnp.int32, (nblk * nblk, width), 0)
     table = jnp.full((nblk * nblk, width), -1.0, jnp.float32)
     for s in range(slots):
-        at = lax.rem(pairs_ref[s, 0], nblk) * nblk + lax.rem(pairs_ref[s, 1], nblk)
+        at = lax.rem(pairs_ref[0, s], nblk) * nblk + lax.rem(pairs_ref[1, s], nblk)
         at = jnp.where(s < count_ref[0, 0], at, -1)
         table = jnp.where(place == at, float(s), table)
     sc[row, pl.ds(slots * width, nblk * nblk), :] = table.astype(jnp.bfloat16)
@@ -70,10 +69,9 @@
 
     pl.semaphore_wait(barrier, len(near))
 
-    waits = {}
     sends = []
     state = {"now": 0.0, "seq": 0, "done": set()}
-    link_free = {}
+    link_free, queues, flying = {}, {}, {}
     heap = []
     actions = {}
     pending = []
@@ -83,28 +81,40 @@
         state["seq"] += 1
         heapq.heappush(heap, (time, kind, state["seq"], name))
 
+    def start(link):
+        while queues[link] and flying[link] < WINDOW[link[0]]:
+            urgent = [e for e in queues[link] if e[0][0] == "S"]
+            entry = urgent[0] if urgent else queues[link][0]
+            queues[link].remove(entry)
+            name, src, dst, dev, nbytes, landed, after = entry
+            flying[link] += 1
+            i = ids.setdefault(name, len(ids))
+            copy = pltpu.make_async_remote_copy(
+                src_ref=src, dst_ref=dst, send_sem=send_sems.at[i], recv_sem=recv_sems.at[i],
+                device_id=dev, device_id_type=MESH,
+            )
+            copy.start()
+            sends.append(copy)
+            rate = RATE[link[0]]
+            t = max(state["now"], link_free.get(link, 0.0)) + nbytes / rate
+            link_free[link] = t
+            actions[name] = (functools.partial(arrive, link, i, landed, dev, after), 0.1)
+            push(t + HOP, 0, name)
+
+    def arrive(link, i, landed, dev, after):
+        pltpu.make_async_remote_copy(
+            src_ref=landed, dst_ref=landed, send_sem=send_sems.at[i], recv_sem=recv_sems.at[i],
+            device_id=dev, device_id_type=MESH,
+        ).wait_recv()
+        flying[link] -= 1
+        if after is not None:
+            after()
+        start(link)
+
     def send(name, src, dst, link, dev, nbytes, landed, after):
-        i = ids.setdefault(name, len(ids))
-        copy = pltpu.make_async_remote_copy(
-            src_ref=src, dst_ref=dst, send_sem=send_sems.at[i], recv_sem=recv_sems.at[i],
-            device_id=dev, device_id_type=MESH,
-        )
-        copy.start()
-        sends.append(copy)
-        rate = CORE if link == "c" else LINK
-        t = max(state["now"], link_free.get(link, 0.0)) + nbytes / rate
-        link_free[link] = t
-
-        def act():
-            pltpu.make_async_remote_copy(
-                src_ref=landed, dst_ref=landed, send_sem=send_sems.at[i], recv_sem=recv_sems.at[i],
-                device_id=dev, device_id_type=MESH,
-            ).wait_recv()
-            if after is not None:
-                after()
-
-        actions[name] = (act, 0.05)
-        push(t + HOP, 0, name)
+        queues.setdefault(link, []).append((name, src, dst, dev, nbytes, landed, after))
+        flying.setdefault(link, 0)
+        start(link)
 
     def step(name, needs, fn, cost):
         actions[name] = (fn, cost)
@@ -135,13 +145,15 @@
         nbytes = ch_rows * tile * 2
 
         def piece(zz, cc, part):
-            r = buf.at[h, wrap(zz, NZ) * 2 + cc]
-            return r if part is None else r.at[pl.ds(part * half, half), :]
+            r = buf.at[wrap(zz, NZ) * 2 + cc]
+            if part is None:
+                return r.at[pl.ds(h * ch_rows, ch_rows), :]
+            return r.at[pl.ds(h * ch_rows + part * half, half), :]
 
         def to_core(name, zz, part):
             src = piece(zz, c, part)
             n = nbytes if part is None else nbytes // 2
-            send(name, src, src, "c", device(dc=1), n, piece(zz, 1 - c, part), None)
+            send(name, src, src, ("c", 0), device(dc=1), n, piece(zz, 1 - c, part), None)
 
         def hop(direction, k):
             part = None if k < NZ // 2 else (0 if direction > 0 else 1)
@@ -167,7 +179,6 @@
 
     def xy_stream(tag, buf, rows, nbytes):
         q = rows // 4
-        names = []
 
         def piece(dx, dy, half, part):
             r = buf.at[wrap(y + dy, NY) * NX + wrap(x + dx, NX)]
@@ -187,7 +198,6 @@
                 land = piece(*off(half, at, -direction * k), half, part)
                 n = nbytes // 2 if k == 1 else nbytes // 4
                 name = (tag, half, 2, at, direction, k)
-                names.append(name)
                 send(name, src, src, (axis, direction), device(**{"d" + axis: direction}), n, land,
                      (lambda: hop(direction, 2)) if k == 1 else None)
 
@@ -204,7 +214,6 @@
                 land = piece(*off(half, -direction * k, 0), half, part)
                 n = nbytes // 2 if k == 1 else nbytes // 4
                 name = (tag, half, 1, direction, k)
-                names.append(name)
 
                 def after():
                     if k == 1:
@@ -224,46 +233,60 @@
             first_phase(half)
         for half in (0, 1):
             second_phase(half, 0)
-        return 80 // 2
+
+    def xy_needs(tag, dx, dy):
+        need = []
+        for half, (first, second) in enumerate(((dx, dy), (dy, dx))):
+            if second == 0:
+                need.extend((tag, half, 1, d, abs(first)) for d in ((1, -1) if first == 2 else (-first,)) if first)
+            else:
+                need.extend((tag, half, 2, first, d, abs(second)) for d in ((1, -1) if second == 2 else (-second,)))
+        return need
 
     def xy_all(tag):
-        need = []
-        for half in (0, 1):
-            for d in (1, -1):
-                for k in (1, 2):
-                    need.append((tag, half, 1, d, k))
-                    need.extend((tag, half, 2, at, d, k) for at in (0, 1, -1, 2))
-        return need
-
-    def expand(first, n):
-        @pl.loop(first, first + n)
-        def _(r):
+        steps = (0, 1, -1, 2)
+        return [n for dx in steps for dy in steps for n in xy_needs(tag, dx, dy)]
+
+    def expand(dxs, dys):
+        strip = width // 2
+
+        @pl.loop(0, len(dxs) * len(dys))
+        def _(i):
+            dx = dxs[0] + (i // len(dys)) * dxs.step
+            dy = dys[0] + lax.rem(i, len(dys)) * dys.step
+            r = wrap(y + dy, NY) * NX + wrap(x + dx, NX)
             t = sc[r, pl.ds(slots * width, nblk * nblk), :].astype(jnp.float32)
-            for b in range(nblk * nblk):
-                line = t[b : b + 1, :]
-                total = jnp.zeros((width, width), jnp.bfloat16)
-                for s in range(slots):
-                    on = jnp.where(line == float(s), 1.0, 0.0).astype(jnp.bfloat16)
-                    total = total + sc[r, pl.ds(s * width, width), :] * on
-                sd[r, pl.ds((b // nblk) * width, width), pl.ds((b % nblk) * width, width)] = total
-
-    def dots(acc, left_buf, right_buf, h, k):
-        far = NZ // 2
-        n = 2 if k in (0, far) else 4
+            for u in range(width // strip):
+                held = [sc[r, pl.ds(s * width + u * strip, strip), :].reshape(strip // 16, 16, width) for s in range(slots)]
+                for b in range(nblk * nblk):
+                    line = jnp.broadcast_to(t[b : b + 1, :], (16, width))
+                    total = None
+                    for s in range(slots):
+                        on = jnp.where(line == float(s), 1.0, 0.0).astype(jnp.bfloat16)
+                        term = held[s] * on[None]
+                        total = term if total is None else total + term
+                    at = (b // nblk) * width + u * strip
+                    sd[r, pl.ds(at, strip), pl.ds((b % nblk) * width, width)] = total.reshape(strip, width)
+
+    def dots(acc, left_buf, right_buf, k, first, rows):
+        n = 2 if k in (0, NZ // 2) else 4
+        span = pl.ds(first, rows)
 
         @pl.loop(0, n)
         def _(i):
             cc = lax.rem(i, 2)
             sign = 1 - 2 * (i // 2)
             t = wrap(z + sign * k, NZ) * 2 + cc
-            acc[h] += jnp.dot(left_buf[h, t], right_buf[t], preferred_element_type=jnp.float32)
+            acc[span, :] += jnp.dot(left_buf[t, span, :], right_buf[t], preferred_element_type=jnp.float32)
 
     def finish_left(h):
-        lr[h, col] = lacc[h].astype(jnp.bfloat16)
+        span = pl.ds(h * ch_rows, ch_rows)
+        lr[col, span, :] = lacc[span, :].astype(jnp.bfloat16)
         z_stream("L", lr, h)
 
     def finish(h):
-        out_ref[pl.ds(h * ch_rows, ch_rows), :] = cacc[h].astype(jnp.bfloat16)
+        span = pl.ds(h * ch_rows, ch_rows)
+        out_ref[span, :] = cacc[span, :].astype(jnp.bfloat16)
 
     lacc[...] = jnp.zeros_like(lacc)
     xy_stream("S", sc, SLOT_ROWS, SLOT_ROWS * width * 2)
@@ -271,18 +294,26 @@
         z_stream("G", gr, h)
     xy_stream("C", gc, tile, tile * tile * 2)
 
-    group = 4
-    for i in range(ROWS // group):
-        step(("expand", i), xy_all("S") + ([("expand", i - 1)] if i else []), functools.partial(expand, i * group, group), 1.0)
-    last = ("expand", ROWS // group - 1)
+    zero, near1, pair, two = range(0, 1), range(-1, 2), range(-1, 2, 2), range(2, 3)
+    shapes = ((near1, zero), (zero, pair), (pair, pair), (two, range(-1, 3)), (near1, two))
+    for i, (dxs, dys) in enumerate(shapes):
+        needs = [n for dx in dxs for dy in dys for n in xy_needs("S", dx, dy)]
+        step(("expand", i), needs, functools.partial(expand, dxs, dys), 0.3 * len(dxs) * len(dys))
+    dense = [("expand", i) for i in range(len(shapes))]
+    both = range(CH)
     far = NZ // 2
-    for h in range(CH):
-        for k in range(far + 1):
-            step(("left", h, k), z_needs("G", h, k) + [last], functools.partial(dots, lacc, gr, sd, h, k), 1.0)
-            step(("prod", h, k), z_needs("L", h, k) + xy_all("C") + [("left done", h)],
-                 functools.partial(dots, cacc, lr, gc, h, k), 1.0)
-        step(("left done", h), [("left", h, k) for k in range(far + 1)], functools.partial(finish_left, h), 0.3)
-        step(("done", h), [("prod", h, k) for k in range(far + 1)], functools.partial(finish, h), 0.3)
+    for k in range(far):
+        needs = [n for h in both for n in z_needs("G", h, k)]
+        step(("left", k), needs + dense, functools.partial(dots, lacc, gr, sd, k, 0, tile), 1.6)
+        needs = [n for h in both for n in z_needs("L", h, k)] + [("left done", h) for h in both]
+        step(("prod", k), needs + xy_all("C"), functools.partial(dots, cacc, lr, gc, k, 0, tile), 1.6)
+    for h in both:
+        step(("left last", h), z_needs("G", h, far) + dense + [("left", k) for k in range(far)],
+             functools.partial(dots, lacc, gr, sd, far, h * ch_rows, ch_rows), 0.6)
+        step(("left done", h), [("left last", h)], functools.partial(finish_left, h), 0.3)
+        step(("prod last", h), z_needs("L", h, far) + [("prod", k) for k in range(far)],
+             functools.partial(dots, cacc, lr, gc, far, h * ch_rows, ch_rows), 0.6)
+        step(("done", h), [("prod last", h)], functools.partial(finish, h), 0.3)
     run()
     for copy in sends:
         copy.wait_send()
@@ -305,13 +336,13 @@
         in_specs=[vmem, vmem, smem, smem, smem],
         out_specs=vmem,
         scratch_shapes=[
-            pltpu.VMEM((CH, COLS, tile // CH, tile), bf),
+            pltpu.VMEM((COLS, tile, tile), bf),
             pltpu.VMEM((ROWS, tile, tile), bf),
-            pltpu.VMEM((CH, COLS, tile // CH, tile), bf),
+            pltpu.VMEM((COLS, tile, tile), bf),
             pltpu.VMEM((ROWS, SLOT_ROWS, width), bf),
             pltpu.VMEM((ROWS, tile, tile), bf),
-            pltpu.VMEM((CH, tile // CH, tile), f32),
-            pltpu.VMEM((CH, tile // CH, tile), f32),
+            pltpu.VMEM((tile, tile), f32),
+            pltpu.VMEM((tile, tile), f32),
             pltpu.SemaphoreType.DMA((N_COPIES,)),
             pltpu.SemaphoreType.DMA((N_COPIES,)),
         ],
@@ -322,7 +353,7 @@
         g0_values,
         sigma_values.reshape(slots * width, width),
         g0_pattern,
-        sigma_pairs.reshape(slots, 2),
+        sigma_pairs.reshape(slots, 2).T,
         sigma_count,
     )
 

time: 137 us -> 101 us (0.74)
  Pallas kernels: 133 us -> 98.3 us
    pallas_call x1, Pallas kernels: 133 us -> 98.3 us  [per_device(): pl.pallas_call(kernel, name='dyson', out_shape=jax.ShapeDtypeStruct((tile...]
where the time goes in v2:
time: 101 us
  Pallas kernels  98.3 us (97%)
  local copies, waits for them, and re-layouts  1.87 us (2%)
    pallas_call x1, Pallas kernels, per_device(): pl.pallas_call(kernel, name='dyson', out_shape=jax.ShapeDtypeStruct((tile...  98.3 us

profile of v2, /device:TPU:1, one launch (start us, length us, event | category | flops | bytes accessed | tf_op | source)
XLA Modules:
  0.0 100.8 jit_solution(2328163568266592574)
XLA Ops:
  0.7 98.3 %dyson.1 = bf16[512,512]{1,0:T(8,128)(2,1)} custom-call(bf16[512,512]{1,0:T(8,128)(2,1)} %g0_ref.1, bf16[768,128]{1,0:T(8,128)(2,1)} %bitcast.4, s32[4,4]{1,0:T(4,128)} %pat_ref.1, s32[2,6]{1,0:T(2,128)} %bitcast.5, s32[1,1]{1,0:T(1,128)S(6)} %copy.7.count_ref), custom_call_target="tpu_custom_call" | custom-call | tf_op jit(solution)/shard_map/dyson/pallas_call | solution.py:332
  98.9 1.9 %copy.8 = bf16[512,512]{1,0:T(8,128)(2,1)} copy(bf16[512,512]{1,0:T(8,128)(2,1)} %dyson.1) | data formatting | bytes 1048576

commit v3 on v2

--- a/solution.py
+++ b/solution.py
@@ -12,23 +12,24 @@
 NX, NY, NZ = 4, 4, 8
 ROWS = NX * NY
 COLS = NZ * 2
-CH = 2
+SPLIT = (192, 320)
+STARTS = (0, 192)
+CH = len(SPLIT)
 SLOT_ROWS = 832
 
 RATE = {"x": 40.0e3, "y": 40.0e3, "z": 46.0e3, "c": 250.0e3}
 HOP = 1.5
-WINDOW = {"x": 2, "y": 2, "z": 99, "c": 99}
+WINDOW = {"x": 2, "y": 2, "z": 2, "c": 99}
 
 
 def kernel(
-    g0_ref, sig_ref, pat_ref, pairs_ref, count_ref, out_ref,
-    gr, gc, lr, sc, sd, lacc, cacc, send_sems, recv_sems,
+    g0_ref, sig_ref, pat_hbm, pairs_hbm, count_ref, out_ref,
+    pat_ref, pairs_ref, raw, gr, gc, lr, sc, sd, lacc, cacc, send_sems, recv_sems, local_sems,
 ):
     tile = g0_ref.shape[0]
     width = sig_ref.shape[1]
     nblk = tile // width
     slots = sig_ref.shape[0] // width
-    ch_rows = tile // CH
     row = lax.axis_index("row")
     col = lax.axis_index("col")
     x, y = lax.rem(row, NX), row // NX
@@ -47,26 +48,39 @@
     for d in near:
         pl.semaphore_signal(barrier, inc=1, device_id=d, device_id_type=MESH)
 
-    for a in range(nblk):
-        for b in range(nblk):
-            ra, rb = pl.ds(a * width, width), pl.ds(b * width, width)
-            block = g0_ref[ra, rb]
-            block = jnp.where(pat_ref[a, b] != 0, block, jnp.zeros_like(block))
-            gc[row, ra, rb] = block
-            gr[col, ra, rb] = block
-            cacc[ra, rb] = block.astype(jnp.float32)
-
-    sc[row, pl.ds(0, slots * width), :] = sig_ref[...]
-    place = lax.broadcasted_iota(jnp.int32, (nblk * nblk, width), 0)
-    table = jnp.full((nblk * nblk, width), -1.0, jnp.float32)
-    for s in range(slots):
-        at = lax.rem(pairs_ref[0, s], nblk) * nblk + lax.rem(pairs_ref[1, s], nblk)
-        at = jnp.where(s < count_ref[0, 0], at, -1)
-        table = jnp.where(place == at, float(s), table)
-    sc[row, pl.ds(slots * width, nblk * nblk), :] = table.astype(jnp.bfloat16)
-    tail = slots * width + nblk * nblk
-    sc[row, pl.ds(tail, SLOT_ROWS - tail), :] = jnp.zeros((SLOT_ROWS - tail, width), jnp.bfloat16)
-
+    load_g0 = pltpu.make_async_copy(g0_ref, raw, local_sems.at[0])
+    load_sig = pltpu.make_async_copy(sig_ref, sc.at[row, pl.ds(0, slots * width), :], local_sems.at[1])
+    small = [
+        pltpu.make_async_copy(src, dst, local_sems.at[2 + i])
+        for i, (src, dst) in enumerate(((pat_hbm, pat_ref), (pairs_hbm, pairs_ref)))
+    ]
+    for copy in (load_g0, *small, load_sig):
+        copy.start()
+
+    def own_blocks():
+        for a in range(nblk):
+            for b in range(nblk):
+                at = (pl.ds(a * width, width), pl.ds(b * width, width))
+                block = raw[at]
+                yield at, jnp.where(pat_ref[a, b] != 0, block, jnp.zeros_like(block))
+
+    def own_table():
+        place = lax.broadcasted_iota(jnp.int32, (nblk * nblk, width), 0)
+        count = jnp.broadcast_to(count_ref[...], place.shape)
+        table = jnp.full((nblk * nblk, width), -1.0, jnp.float32)
+        for s in range(slots):
+            at = lax.rem(pairs_ref[0, s], nblk) * nblk + lax.rem(pairs_ref[1, s], nblk)
+            table = jnp.where((place == at) & (s < count), float(s), table)
+        sc[row, pl.ds(slots * width, nblk * nblk), :] = table.astype(jnp.bfloat16)
+        tail = slots * width + nblk * nblk
+        sc[row, pl.ds(tail, SLOT_ROWS - tail), :] = jnp.zeros((SLOT_ROWS - tail, width), jnp.bfloat16)
+
+    for copy in small:
+        copy.wait()
+    own_table()
+    load_g0.wait()
+    for at, block in own_blocks():
+        gr[(col, *at)] = block
     pl.semaphore_wait(barrier, len(near))
 
     sends = []
@@ -81,10 +95,14 @@
         state["seq"] += 1
         heapq.heappush(heap, (time, kind, state["seq"], name))
 
+    def urgency(name):
+        if name[0] == "G":
+            return name[2]
+        return {"S": 0, "C": 1, "L": CH}[name[0]]
+
     def start(link):
         while queues[link] and flying[link] < WINDOW[link[0]]:
-            urgent = [e for e in queues[link] if e[0][0] == "S"]
-            entry = urgent[0] if urgent else queues[link][0]
+            entry = min(queues[link], key=lambda e: urgency(e[0]))
             queues[link].remove(entry)
             name, src, dst, dev, nbytes, landed, after = entry
             flying[link] += 1
@@ -141,14 +159,14 @@
         assert not pending, pending
 
     def z_stream(tag, buf, h):
-        half = ch_rows // 2
-        nbytes = ch_rows * tile * 2
+        half = SPLIT[h] // 2
+        nbytes = SPLIT[h] * tile * 2
 
         def piece(zz, cc, part):
             r = buf.at[wrap(zz, NZ) * 2 + cc]
             if part is None:
-                return r.at[pl.ds(h * ch_rows, ch_rows), :]
-            return r.at[pl.ds(h * ch_rows + part * half, half), :]
+                return r.at[pl.ds(STARTS[h], SPLIT[h]), :]
+            return r.at[pl.ds(STARTS[h] + part * half, half), :]
 
         def to_core(name, zz, part):
             src = piece(zz, c, part)
@@ -280,19 +298,24 @@
             acc[span, :] += jnp.dot(left_buf[t, span, :], right_buf[t], preferred_element_type=jnp.float32)
 
     def finish_left(h):
-        span = pl.ds(h * ch_rows, ch_rows)
+        span = pl.ds(STARTS[h], SPLIT[h])
         lr[col, span, :] = lacc[span, :].astype(jnp.bfloat16)
         z_stream("L", lr, h)
 
     def finish(h):
-        span = pl.ds(h * ch_rows, ch_rows)
+        span = pl.ds(STARTS[h], SPLIT[h])
         out_ref[span, :] = cacc[span, :].astype(jnp.bfloat16)
 
-    lacc[...] = jnp.zeros_like(lacc)
-    xy_stream("S", sc, SLOT_ROWS, SLOT_ROWS * width * 2)
     for h in range(CH):
         z_stream("G", gr, h)
+    load_sig.wait()
+    xy_stream("S", sc, SLOT_ROWS, SLOT_ROWS * width * 2)
+    for at, block in own_blocks():
+        gc[(row, *at)] = block
     xy_stream("C", gc, tile, tile * tile * 2)
+    for at, block in own_blocks():
+        cacc[at] = block.astype(jnp.float32)
+    lacc[...] = jnp.zeros_like(lacc)
 
     zero, near1, pair, two = range(0, 1), range(-1, 2), range(-1, 2, 2), range(2, 3)
     shapes = ((near1, zero), (zero, pair), (pair, pair), (two, range(-1, 3)), (near1, two))
@@ -303,16 +326,17 @@
     both = range(CH)
     far = NZ // 2
     for k in range(far):
-        needs = [n for h in both for n in z_needs("G", h, k)]
-        step(("left", k), needs + dense, functools.partial(dots, lacc, gr, sd, k, 0, tile), 1.6)
+        for h in both:
+            step(("left", h, k), z_needs("G", h, k) + dense,
+                 functools.partial(dots, lacc, gr, sd, k, STARTS[h], SPLIT[h]), 0.8)
         needs = [n for h in both for n in z_needs("L", h, k)] + [("left done", h) for h in both]
         step(("prod", k), needs + xy_all("C"), functools.partial(dots, cacc, lr, gc, k, 0, tile), 1.6)
     for h in both:
-        step(("left last", h), z_needs("G", h, far) + dense + [("left", k) for k in range(far)],
-             functools.partial(dots, lacc, gr, sd, far, h * ch_rows, ch_rows), 0.6)
+        step(("left last", h), z_needs("G", h, far) + dense + [("left", h, k) for k in range(far)],
+             functools.partial(dots, lacc, gr, sd, far, STARTS[h], SPLIT[h]), 0.6)
         step(("left done", h), [("left last", h)], functools.partial(finish_left, h), 0.3)
         step(("prod last", h), z_needs("L", h, far) + [("prod", k) for k in range(far)],
-             functools.partial(dots, cacc, lr, gc, far, h * ch_rows, ch_rows), 0.6)
+             functools.partial(dots, cacc, lr, gc, far, STARTS[h], SPLIT[h]), 0.6)
         step(("done", h), [("prod last", h)], functools.partial(finish, h), 0.3)
     run()
     for copy in sends:
@@ -327,15 +351,17 @@
     tile = g0_values.shape[0]
     _, slots, width, _ = sigma_values.shape
     bf, f32 = jnp.bfloat16, jnp.float32
-    vmem = pl.BlockSpec(memory_space=pltpu.VMEM)
-    smem = pl.BlockSpec(memory_space=pltpu.SMEM)
+    hbm = pl.BlockSpec(memory_space=pltpu.HBM)
     return pl.pallas_call(
         kernel,
         name="dyson",
-        out_shape=jax.ShapeDtypeStruct((tile, tile), bf),
-        in_specs=[vmem, vmem, smem, smem, smem],
-        out_specs=vmem,
+        out_shape=pltpu.VMEM((tile, tile), bf),
+        in_specs=[hbm] * 4 + [pl.BlockSpec(memory_space=pltpu.VMEM)],
+        out_specs=pl.BlockSpec(memory_space=pltpu.VMEM),
         scratch_shapes=[
+            pltpu.SMEM(g0_pattern.shape, jnp.int32),
+            pltpu.SMEM((2, slots), jnp.int32),
+            pltpu.VMEM((tile, tile), bf),
             pltpu.VMEM((COLS, tile, tile), bf),
             pltpu.VMEM((ROWS, tile, tile), bf),
             pltpu.VMEM((COLS, tile, tile), bf),
@@ -345,6 +371,7 @@
             pltpu.VMEM((tile, tile), f32),
             pltpu.SemaphoreType.DMA((N_COPIES,)),
             pltpu.SemaphoreType.DMA((N_COPIES,)),
+            pltpu.SemaphoreType.DMA((5,)),
         ],
         compiler_params=pltpu.CompilerParams(
             collective_id=0, has_side_effects=True, vmem_limit_bytes=58 << 20

time: 101 us -> 98.2 us (0.972)
  Pallas kernels: 98.3 us -> 96.7 us
  local copies, waits for them, and re-layouts: 1.87 us -> 0.8 us
    pallas_call x1, Pallas kernels: 98.3 us -> 96.7 us  [per_device(): pl.pallas_call(kernel, name='dyson', out_shape=pltpu.VMEM((tile, tile), b...]
    unnamed x1, local copies, waits for them, and re-layouts: 1.87 us -> 0.8 us
where the time goes in v3:
time: 98.2 us; the launch traced here: 98.1 us
  Pallas kernels  96.7 us (98%)
    pallas_call x1, Pallas kernels, per_device(): pl.pallas_call(kernel, name='dyson', out_shape=pltpu.VMEM((tile, tile), b...  96.7 us

profile of v3, /device:TPU:1, one launch (start us, length us, event | category | flops | bytes accessed | tf_op | source)
XLA Modules:
  0.0 98.1 jit_solution(11633526609894748686)
XLA Ops:
  0.7 96.7 %dyson.1 = bf16[512,512]{1,0:T(8,128)(2,1)S(1)} custom-call(bf16[512,512]{1,0:T(8,128)(2,1)} %g0_ref.1, bf16[768,128]{1,0:T(8,128)(2,1)} %bitcast.4, s32[4,4]{1,0:T(4,128)} %pat_hbm.1, s32[2,6]{1,0:T(2,128)} %bitcast.5, s32[1,1]{1,0:T(1,128)S(6)} %copy.8.count_ref), custom_call_target="tpu_custom_call" | custom-call | tf_op jit(solution)/shard_map/dyson/pallas_call | solution.py:355
  97.3 0.8 copy.7

commit v4 on v3

--- a/solution.py
+++ b/solution.py
@@ -77,15 +77,14 @@
 
     for copy in small:
         copy.wait()
-    own_table()
     load_g0.wait()
     for at, block in own_blocks():
         gr[(col, *at)] = block
     pl.semaphore_wait(barrier, len(near))
 
-    sends = []
+    sends = {}
     state = {"now": 0.0, "seq": 0, "done": set()}
-    link_free, queues, flying = {}, {}, {}
+    link_free, queues, flying, landed_on = {}, {}, {}, {}
     heap = []
     actions = {}
     pending = []
@@ -112,7 +111,7 @@
                 device_id=dev, device_id_type=MESH,
             )
             copy.start()
-            sends.append(copy)
+            sends[link].append(copy)
             rate = RATE[link[0]]
             t = max(state["now"], link_free.get(link, 0.0)) + nbytes / rate
             link_free[link] = t
@@ -125,13 +124,17 @@
             device_id=dev, device_id_type=MESH,
         ).wait_recv()
         flying[link] -= 1
+        landed_on[link] = landed_on.get(link, 0) + 1
         if after is not None:
             after()
         start(link)
+        if landed_on[link] > 2:
+            sends[link].pop(0).wait_send()
 
     def send(name, src, dst, link, dev, nbytes, landed, after):
         queues.setdefault(link, []).append((name, src, dst, dev, nbytes, landed, after))
         flying.setdefault(link, 0)
+        sends.setdefault(link, [])
         start(link)
 
     def step(name, needs, fn, cost):
@@ -286,8 +289,13 @@
                     at = (b // nblk) * width + u * strip
                     sd[r, pl.ds(at, strip), pl.ds((b % nblk) * width, width)] = total.reshape(strip, width)
 
+    def far_dot(acc, left_buf, right_buf, cc, h):
+        span = pl.ds(STARTS[h], SPLIT[h])
+        t = wrap(z + NZ // 2, NZ) * 2 + cc
+        acc[span, :] += jnp.dot(left_buf[t, span, :], right_buf[t], preferred_element_type=jnp.float32)
+
     def dots(acc, left_buf, right_buf, k, first, rows):
-        n = 2 if k in (0, NZ // 2) else 4
+        n = 2 if k == 0 else 4
         span = pl.ds(first, rows)
 
         @pl.loop(0, n)
@@ -308,6 +316,7 @@
 
     for h in range(CH):
         z_stream("G", gr, h)
+    own_table()
     load_sig.wait()
     xy_stream("S", sc, SLOT_ROWS, SLOT_ROWS * width * 2)
     for at, block in own_blocks():
@@ -332,15 +341,19 @@
         needs = [n for h in both for n in z_needs("L", h, k)] + [("left done", h) for h in both]
         step(("prod", k), needs + xy_all("C"), functools.partial(dots, cacc, lr, gc, k, 0, tile), 1.6)
     for h in both:
-        step(("left last", h), z_needs("G", h, far) + dense + [("left", h, k) for k in range(far)],
-             functools.partial(dots, lacc, gr, sd, far, STARTS[h], SPLIT[h]), 0.6)
-        step(("left done", h), [("left last", h)], functools.partial(finish_left, h), 0.3)
-        step(("prod last", h), z_needs("L", h, far) + [("prod", k) for k in range(far)],
-             functools.partial(dots, cacc, lr, gc, far, STARTS[h], SPLIT[h]), 0.6)
-        step(("done", h), [("prod last", h)], functools.partial(finish, h), 0.3)
+        for who, cc in (("z", c), ("c", 1 - c)):
+            got = [("G", who, h, d, far) for d in (1, -1)]
+            step(("left last", h, who), got + dense + [("left", h, k) for k in range(far)],
+                 functools.partial(far_dot, lacc, gr, sd, cc, h), 0.4)
+            got = [("L", who, h, d, far) for d in (1, -1)]
+            step(("prod last", h, who), got + [("prod", k) for k in range(far)],
+                 functools.partial(far_dot, cacc, lr, gc, cc, h), 0.4)
+        step(("left done", h), [("left last", h, who) for who in ("z", "c")], functools.partial(finish_left, h), 0.3)
+        step(("done", h), [("prod last", h, who) for who in ("z", "c")], functools.partial(finish, h), 0.3)
     run()
-    for copy in sends:
-        copy.wait_send()
+    for left_over in sends.values():
+        for copy in left_over:
+            copy.wait_send()
     assert len(ids) == N_COPIES, len(ids)
 
 

time: 98.2 us -> 97.4 us (level)
  no operation moved by 1% of the time
where the time goes in v4:
time: 97.4 us; the launch traced here: 97.3 us
  Pallas kernels  95.8 us (98%)
    pallas_call x1, Pallas kernels, per_device(): pl.pallas_call(kernel, name='dyson', out_shape=pltpu.VMEM((tile, tile), b...  95.8 us

profile of v4, /device:TPU:1, one launch (start us, length us, event | category | flops | bytes accessed | tf_op | source)
XLA Modules:
  0.0 97.3 jit_solution(15453417406956064379)
XLA Ops:
  0.7 95.8 %dyson.1 = bf16[512,512]{1,0:T(8,128)(2,1)S(1)} custom-call(bf16[512,512]{1,0:T(8,128)(2,1)} %g0_ref.1, bf16[768,128]{1,0:T(8,128)(2,1)} %bitcast.4, s32[4,4]{1,0:T(4,128)} %pat_hbm.1, s32[2,6]{1,0:T(2,128)} %bitcast.5, s32[1,1]{1,0:T(1,128)S(6)} %copy.8.count_ref), custom_call_target="tpu_custom_call" | custom-call | tf_op jit(solution)/shard_map/dyson/pallas_call | solution.py:368
  96.5 0.8 copy.7

commit v5 on v4

--- a/solution.py
+++ b/solution.py
@@ -12,8 +12,8 @@
 NX, NY, NZ = 4, 4, 8
 ROWS = NX * NY
 COLS = NZ * 2
-SPLIT = (192, 320)
-STARTS = (0, 192)
+SPLIT = (224, 288)
+STARTS = (0, 224)
 CH = len(SPLIT)
 SLOT_ROWS = 832
 
@@ -48,17 +48,21 @@
     for d in near:
         pl.semaphore_signal(barrier, inc=1, device_id=d, device_id_type=MESH)
 
-    load_g0 = pltpu.make_async_copy(g0_ref, raw, local_sems.at[0])
-    load_sig = pltpu.make_async_copy(sig_ref, sc.at[row, pl.ds(0, slots * width), :], local_sems.at[1])
+    top = tile // 2
+    load_g0 = [
+        pltpu.make_async_copy(g0_ref.at[pl.ds(i * top, top), :], raw.at[pl.ds(i * top, top), :], local_sems.at[i])
+        for i in range(2)
+    ]
+    load_sig = pltpu.make_async_copy(sig_ref, sc.at[row, pl.ds(0, slots * width), :], local_sems.at[4])
     small = [
         pltpu.make_async_copy(src, dst, local_sems.at[2 + i])
         for i, (src, dst) in enumerate(((pat_hbm, pat_ref), (pairs_hbm, pairs_ref)))
     ]
-    for copy in (load_g0, *small, load_sig):
+    for copy in (load_g0[0], *small, load_g0[1], load_sig):
         copy.start()
 
-    def own_blocks():
-        for a in range(nblk):
+    def own_blocks(block_rows=range(nblk)):
+        for a in block_rows:
             for b in range(nblk):
                 at = (pl.ds(a * width, width), pl.ds(b * width, width))
                 block = raw[at]
@@ -77,8 +81,8 @@
 
     for copy in small:
         copy.wait()
-    load_g0.wait()
-    for at, block in own_blocks():
+    load_g0[0].wait()
+    for at, block in own_blocks(range(nblk // 2)):
         gr[(col, *at)] = block
     pl.semaphore_wait(barrier, len(near))
 
@@ -314,8 +318,11 @@
         span = pl.ds(STARTS[h], SPLIT[h])
         out_ref[span, :] = cacc[span, :].astype(jnp.bfloat16)
 
-    for h in range(CH):
-        z_stream("G", gr, h)
+    z_stream("G", gr, 0)
+    load_g0[1].wait()
+    for at, block in own_blocks(range(nblk // 2, nblk)):
+        gr[(col, *at)] = block
+    z_stream("G", gr, 1)
     own_table()
     load_sig.wait()
     xy_stream("S", sc, SLOT_ROWS, SLOT_ROWS * width * 2)

time: 97.4 us -> 97.4 us (level)
  no operation moved by 1% of the time
where the time goes in v5:
time: 97.4 us; the launch traced here: 97.3 us
  Pallas kernels  95.8 us (98%)
    pallas_call x1, Pallas kernels, per_device(): pl.pallas_call(kernel, name='dyson', out_shape=pltpu.VMEM((tile, tile), b...  95.8 us

profile of v5, /device:TPU:1, one launch (start us, length us, event | category | flops | bytes accessed | tf_op | source)
XLA Modules:
  0.0 97.3 jit_solution(12228114198601215043)
XLA Ops:
  0.7 95.8 %dyson.1 = bf16[512,512]{1,0:T(8,128)(2,1)S(1)} custom-call(bf16[512,512]{1,0:T(8,128)(2,1)} %g0_ref.1, bf16[768,128]{1,0:T(8,128)(2,1)} %bitcast.4, s32[4,4]{1,0:T(4,128)} %pat_hbm.1, s32[2,6]{1,0:T(2,128)} %bitcast.5, s32[1,1]{1,0:T(1,128)S(6)} %copy.8.count_ref), custom_call_target="tpu_custom_call" | custom-call | tf_op jit(solution)/shard_map/dyson/pallas_call | solution.py:375
  96.5 0.8 copy.7

commit v6 on v5

--- a/solution.py
+++ b/solution.py
@@ -175,10 +175,12 @@
                 return r.at[pl.ds(STARTS[h], SPLIT[h]), :]
             return r.at[pl.ds(STARTS[h] + part * half, half), :]
 
-        def to_core(name, zz, part):
-            src = piece(zz, c, part)
-            n = nbytes if part is None else nbytes // 2
-            send(name, src, src, ("c", 0), device(dc=1), n, piece(zz, 1 - c, part), None)
+        def to_core(name, zz, part, first=0, rows=None):
+            src, land = piece(zz, c, part), piece(zz, 1 - c, part)
+            if rows is not None:
+                src, land = src.at[pl.ds(first, rows), :], land.at[pl.ds(first, rows), :]
+            n = (rows or SPLIT[h]) * tile * 2
+            send(name, src, src, ("c", 0), device(dc=1), n, land, None)
 
         def hop(direction, k):
             part = None if k < NZ // 2 else (0 if direction > 0 else 1)
@@ -188,7 +190,12 @@
             def after():
                 if k < NZ // 2:
                     hop(direction, k + 1)
-                to_core((tag, "c", h, direction, k), z - direction * k, part)
+                if part is None:
+                    to_core((tag, "c", h, direction, k), z - direction * k, part)
+                else:
+                    cut = half // 32 * 16
+                    to_core((tag, "c", h, direction, k), z - direction * k, part, 0, cut)
+                    to_core((tag, "c2", h, direction, k), z - direction * k, part, cut, half - cut)
 
             send((tag, "z", h, direction, k), src, src, ("z", direction), device(dz=direction), n,
                  piece(z - direction * k, c, part), after)
@@ -348,11 +355,12 @@
         needs = [n for h in both for n in z_needs("L", h, k)] + [("left done", h) for h in both]
         step(("prod", k), needs + xy_all("C"), functools.partial(dots, cacc, lr, gc, k, 0, tile), 1.6)
     for h in both:
+        parts_of = {"z": ("z",), "c": ("c", "c2")}
         for who, cc in (("z", c), ("c", 1 - c)):
-            got = [("G", who, h, d, far) for d in (1, -1)]
+            got = [("G", w, h, d, far) for d in (1, -1) for w in parts_of[who]]
             step(("left last", h, who), got + dense + [("left", h, k) for k in range(far)],
                  functools.partial(far_dot, lacc, gr, sd, cc, h), 0.4)
-            got = [("L", who, h, d, far) for d in (1, -1)]
+            got = [("L", w, h, d, far) for d in (1, -1) for w in parts_of[who]]
             step(("prod last", h, who), got + [("prod", k) for k in range(far)],
                  functools.partial(far_dot, cacc, lr, gc, cc, h), 0.4)
         step(("left done", h), [("left last", h, who) for who in ("z", "c")], functools.partial(finish_left, h), 0.3)
@@ -364,7 +372,7 @@
     assert len(ids) == N_COPIES, len(ids)
 
 
-N_COPIES = 2 * 40 + 2 * CH * (2 * (NZ // 2) * 2 + 1)
+N_COPIES = 2 * 40 + 2 * CH * (2 * (NZ // 2) * 2 + 1 + 2)
 
 
 def per_device(g0_values, g0_pattern, sigma_values, sigma_pairs, sigma_count):

time: 97.4 us -> 97.6 us (level)
  no operation moved by 1% of the time
where the time goes in v6:
time: 97.6 us; the launch traced here: 97.5 us
  Pallas kernels  96.1 us (98%)
    pallas_call x1, Pallas kernels, per_device(): pl.pallas_call(kernel, name='dyson', out_shape=pltpu.VMEM((tile, tile), b...  96.1 us

profile of v6, /device:TPU:1, one launch (start us, length us, event | category | flops | bytes accessed | tf_op | source)
XLA Modules:
  0.0 97.5 jit_solution(17656878605299799300)
XLA Ops:
  0.7 96.1 %dyson.1 = bf16[512,512]{1,0:T(8,128)(2,1)S(1)} custom-call(bf16[512,512]{1,0:T(8,128)(2,1)} %g0_ref.1, bf16[768,128]{1,0:T(8,128)(2,1)} %bitcast.4, s32[4,4]{1,0:T(4,128)} %pat_hbm.1, s32[2,6]{1,0:T(2,128)} %bitcast.5, s32[1,1]{1,0:T(1,128)S(6)} %copy.8.count_ref), custom_call_target="tpu_custom_call" | custom-call | tf_op jit(solution)/shard_map/dyson/pallas_call | solution.py:383
  96.8 0.8 copy.7
